TPU v7x, 32 devices: a whole 2x2x4 slice. The times are simulated.
32 devices in a mesh: qrow: 8 (over z, x), kcol: 4 (over y, core).
Axes of the slice: x: 2, y: 2, z: 4, core: 2. Of those that a mesh axis runs over, the one named last changes fastest.
Arguments:
- queries: bfloat16 [128, 8192], P(('qrow', 'kcol')), may hold values from -200 to 200
- keys_values: bfloat16 [2, 4096, 512], P(None, ('kcol', 'qrow')), may hold values from -8 to 8
- doc_blocks: int32 [32], replicated, may hold values from 0 to 1, never falling along the last dimension, each value on 1 to 17 neighbouring positions
Outputs:
- attended: bfloat16 [128, 8192], P(('qrow', 'kcol'))
Inputs may be any that keep to these rules, and one draw needn't show every extreme that they name: doc_blocks[b] is the document of positions 128 b to 128 b + 127; each document covers 1 to 17 consecutive entries (blocks), one document exactly that many.
All inputs are finite; a program needn't handle non-finite values.
Results may differ from a plain program's by a relative error of at most 0.0046.
Values may be sent and summed in bfloat16 or wider, within the bound.
A program may use at most 128 MiB of HBM per device.

v0:
```python
import math

import jax
import jax.numpy as jnp
from jax import lax
from jax.sharding import PartitionSpec as P

QUERY_HEADS = 64
KEY_VALUE_HEADS = 4
HEAD_WIDTH = 128


masked_score = -1e30


def joined(part, axis, combine):
    gathered = jax.tree.map(lambda a: lax.all_gather(a, axis), part)

    def take(source):
        return jax.tree.map(lambda a: lax.dynamic_index_in_dim(a, source, 0, False), gathered)

    return lax.fori_loop(
        1, lax.axis_size(axis), lambda source, state: combine(state, take(source)), take(0)
    )


def combine_parts(first, second):
    max_one, sum_one, out_one = first
    max_two, sum_two, out_two = second
    top_max = jnp.maximum(max_one, max_two)
    scale_one = jnp.exp(max_one - top_max)
    scale_two = jnp.exp(max_two - top_max)
    height = out_one.shape[0]
    merged = (
        out_one.reshape(height, QUERY_HEADS, HEAD_WIDTH) * scale_one[:, :, None]
        + out_two.reshape(height, QUERY_HEADS, HEAD_WIDTH) * scale_two[:, :, None]
    )
    return (
        top_max,
        sum_one * scale_one + sum_two * scale_two,
        merged.reshape(height, QUERY_HEADS * HEAD_WIDTH),
    )


def per_device(queries, keys_values, doc_blocks):
    local_rows = queries.shape[0]
    row_block = lax.all_gather(queries, "kcol", axis=0, tiled=True)
    key_block = lax.all_gather(keys_values, "qrow", axis=1, tiled=True)
    block_rows = row_block.shape[0]
    range_keys = key_block.shape[1]
    total_queries = block_rows * lax.axis_size("qrow")
    total_keys = range_keys * lax.axis_size("kcol")
    stripe_len = total_keys * 128 // total_queries
    stripe_blocks = stripe_len // 128
    query_index = lax.axis_index("qrow") * block_rows + jnp.arange(block_rows, dtype=jnp.int32)
    query_pos = query_index // 128 * stripe_len + stripe_len - 128 + query_index % 128
    doc_slot = query_index // 128 * stripe_blocks + stripe_blocks - 1
    onehot = doc_slot[:, None] == jnp.arange(doc_blocks.shape[0], dtype=jnp.int32)[None, :]
    query_doc = jnp.sum(jnp.where(onehot, doc_blocks[None, :], 0), axis=1)
    key_first = lax.axis_index("kcol") * range_keys
    key_pos = key_first + jnp.arange(range_keys, dtype=jnp.int32)
    key_doc = jnp.repeat(
        lax.dynamic_slice_in_dim(doc_blocks, key_first // 128, range_keys // 128, 0), 128
    )
    live_mask = (query_doc[:, None] == key_doc[None, :]) & (key_pos[None, :] <= query_pos[:, None])
    query_group_width = QUERY_HEADS // KEY_VALUE_HEADS
    score_scale = 1.0 / math.sqrt(HEAD_WIDTH)
    out_list = []
    max_list = []
    sum_list = []
    for query_head_group in range(KEY_VALUE_HEADS):
        grouped = row_block[
            :,
            query_head_group
            * query_group_width
            * HEAD_WIDTH : (query_head_group + 1)
            * query_group_width
            * HEAD_WIDTH,
        ].reshape(block_rows, query_group_width, HEAD_WIDTH)
        key_part = key_block[
            0, :, query_head_group * HEAD_WIDTH : (query_head_group + 1) * HEAD_WIDTH
        ]
        value_part = key_block[
            1, :, query_head_group * HEAD_WIDTH : (query_head_group + 1) * HEAD_WIDTH
        ]
        scores = (
            jnp.einsum("qhd,kd->hqk", grouped, key_part, preferred_element_type=jnp.float32)
            * score_scale
        )
        scores = jnp.where(live_mask[None], scores, masked_score)
        row_max = jnp.max(scores, axis=2)
        weights = jnp.where(live_mask[None], jnp.exp(scores - row_max[:, :, None]), 0.0)
        row_sum = jnp.sum(weights, axis=2)
        partial_value = jnp.einsum(
            "hqk,kd->qhd",
            weights.astype(jnp.bfloat16),
            value_part,
            preferred_element_type=jnp.float32,
        )
        out_list.append(partial_value)
        max_list.append(row_max.T)
        sum_list.append(row_sum.T)
    part_out = jnp.concatenate(out_list, axis=1).reshape(block_rows, QUERY_HEADS * HEAD_WIDTH)
    part_max = jnp.concatenate(max_list, axis=1)
    part_sum = jnp.concatenate(sum_list, axis=1)
    merged_max, merged_sum, merged_out = joined(
        (part_max, part_sum, part_out), "kcol", combine_parts
    )
    first_row = lax.axis_index("kcol") * local_rows
    own_out = lax.dynamic_slice_in_dim(merged_out, first_row, local_rows, 0)
    own_sum = lax.dynamic_slice_in_dim(merged_sum, first_row, local_rows, 0)
    result = own_out.reshape(local_rows, QUERY_HEADS, HEAD_WIDTH) / own_sum[:, :, None]
    return result.reshape(local_rows, QUERY_HEADS * HEAD_WIDTH).astype(jnp.bfloat16)


def solution(mesh):
    in_specs = (P(("qrow", "kcol"), None), P(None, ("kcol", "qrow"), None), P())
    out_specs = P(("qrow", "kcol"), None)
    return jax.shard_map(
        per_device, mesh=mesh, in_specs=in_specs, out_specs=out_specs, check_vma=False
    )
```

profile of v0, /device:TPU:0, one launch (start us, length us, event | category | flops | bytes accessed | tf_op | source)
XLA Modules:
  0.0 106.0 jit_solution(15865848161103199110)
XLA Ops:
  6.5 0.7 all-gather.6.cloned.1.call-update
  7.3 7.5 %all-gather.2 = bf16[4,4,8192]{2,1,0:T(4,128)(2,1)S(1)} all-gather(bf16[1,4,8192]{2,1,0:T(4,128)(2,1)} %bitcast.148), channel_id=1, replica_groups=mesh['qrow'=8,'kcol'=4] {'kcol'}, dimensions={0}, use_global_device_ids=true | all-gather | bytes 327680 | tf_op jit(solution)/shard_map/all_gather | solution.py:47
  15.5 45.9 %all-gather.6.cloned.1.call-done = bf16[2,1024,512]{2,1,0:T(8,128)(2,1)} async-done(((bf16[2,128,512]{2,1,0:T(8,128)(2,1)}), bf16[2,1024,512]{2,1,0:T(8,128)(2,1)}) %all-gather.6.cloned.1.call-update) | async-done | bytes 2097168 | tf_op jit(solution)/shard_map/all_gather | solution.py:48
  61.3 1.5 %fusion.42 = (f32[16,16]{0,1:T(8,128)S(1)}, f32[16,16,1024]{2,0,1:T(8,128)S(1)}) fusion(bf16[16,16,128]{2,1,0:T(8,128)(2,1)S(1)} %bitcast.138, bf16[2,1024,512]{2,1,0:T(8,128)(2,1)} %all-gather.6.cloned.1.call-done, pred[16,1024]{1,0:T(8,128)(4,1)S(1)} %compare_and_fusion), kind=kOutput, calls=%fused_computation.86 | convolution fusion | flops 67895040 | bytes 1393664 | tf_op jit(solution)/shard_map/qhd,kd->hqk/dot_general | solution.py:87
  62.8 1.3 %fusion.43 = (f32[16,16]{0,1:T(8,128)S(1)}, f32[16,16,1024]{2,0,1:T(8,128)S(1)}) fusion(bf16[16,16,128]{2,1,0:T(8,128)(2,1)S(1)} %bitcast.141, bf16[2,1024,512]{2,1,0:T(8,128)(2,1)} %all-gather.6.cloned.1.call-done, pred[16,1024]{1,0:T(8,128)(4,1)S(1)} %compare_and_fusion), kind=kOutput, calls=%fused_computation.87 | convolution fusion | flops 67895040 | bytes 1393664 | tf_op jit(solution)/shard_map/qhd,kd->hqk/dot_general | solution.py:87
  64.2 0.4 fusion.44
  64.6 0.4 fusion.45
  65.0 0.4 convolution_bitcast_fusion
  65.4 0.4 convolution_bitcast_fusion.1
  65.8 0.4 convolution_bitcast_fusion.2
  66.2 0.4 convolution_bitcast_fusion.3
  66.6 0.8 pad_maximum_fusion
  67.4 1.9 %all_gather_reshape.3 = f32[1,16,8192]{2,1,0:T(8,128)} reshape(f32[16,64,128]{2,1,0:T(8,128)} %pad_maximum_fusion) | data formatting | bytes 1048576 | tf_op jit(solution)/shard_map/all_gather;reshape | solution.py:17
  69.5 5.2 %all-gather = f32[64,64]{1,0:T(8,128)S(1)} all-gather(f32[16,64]{1,0:T(8,128)S(1)} %pad_maximum_fusion.1), channel_id=2, replica_groups=mesh['qrow'=8,'kcol'=4] {'kcol'}, dimensions={0}, use_global_device_ids=true | all-gather | bytes 20480 | tf_op jit(solution)/shard_map/all_gather | solution.py:17
  74.7 2.3 %fusion.12 = (f32[16,16]{0,1:T(8,128)S(1)}, f32[16,16]{0,1:T(8,128)S(1)}, f32[16,16]{0,1:T(8,128)S(1)}, f32[16,16]{0,1:T(8,128)S(1)}) fusion(f32[16,16,1024]{2,0,1:T(8,128)} %copy-done, f32[16,16]{0,1:T(8,128)S(1)} %get-tuple-element.216, pred[16,1024]{1,0:T(8,128)(4,1)S(1)} %compare_and_fusion, f32[16,16,1024]{2,0,1:T(8,128)S(1)} %get-tuple-element.215, ...), kind=kLoop, calls=%fused_computation.30 | loop fusion | flops 3144704 | bytes 4218880 | tf_op jit(solution)/shard_map/reduce_sum | solution.py:93
  77.1 5.5 %all-gather.1 = f32[64,64]{1,0:T(8,128)S(1)} all-gather(f32[16,64]{1,0:T(8,128)S(1)} %pad_maximum_fusion.2), channel_id=3, replica_groups=mesh['qrow'=8,'kcol'=4] {'kcol'}, dimensions={0}, use_global_device_ids=true | all-gather | bytes 20480 | tf_op jit(solution)/shard_map/all_gather | solution.py:17
  82.5 8.3 %all-gather.8.cloned.1.call-done = f32[4,16,8192]{2,1,0:T(8,128)} async-done(((f32[1,16,8192]{2,1,0:T(8,128)}), f32[4,16,8192]{2,1,0:T(8,128)}) %all-gather.8.cloned.1.call-update) | async-done | bytes 2097168 | tf_op jit(solution)/shard_map/all_gather | solution.py:17
  90.8 1.1 %slice_bitcast_fusion = f32[16,8192]{1,0:T(8,128)S(1)} fusion(f32[4,16,8192]{2,1,0:T(8,128)} %all-gather.8.cloned.1.call-done), kind=kLoop, calls=%fused_computation.37 | loop fusion | bytes 1048576 | tf_op jit(solution)/shard_map/jit(dynamic_index_in_dim)/squeeze | solution.py:20
  91.9 6.4 %while.19 = (s32[]{:T(128)}, f32[16,64]{1,0:T(8,128)S(1)}, f32[16,64]{1,0:T(8,128)S(1)}, f32[16,8192]{1,0:T(8,128)S(1)}, f32[4,16,64]{2,1,0:T(8,128)S(1)}, /*ind...) while((s32[]{:T(128)}, f32[16,64]{1,0:T(8,128)S(1)}, ...), condition=%wide.region_10.11_spmd, body=%wide.region_9.10_spmd.sunk | while | flops 399365 | bytes 3711127 | solution.py:22
  92.2 0.2 mul.171
  92.4 1.7 %fusion.53 = f32[16,8192]{1,0:T(8,128)S(1)} fusion(f32[2,8,64,128]{3,2,1,0:T(8,128)S(1)} %bitcast.136, f32[16,8192]{1,0:T(8,128)S(1)} %get-tuple-element.282, f32[2,8,64,128]{3,2,1,0:T(8,128)S(1)} %bitcast.137, f32[4,16,8192]{2,1,0:T(8,128)} %get-tuple-element.295, s32[]{:T(128)S(6)} %select_n.133), kind=kLoop, calls=%fused_computation.1.clone.1 | loop fusion | flops 393216 | bytes 2621444 | tf_op jit(solution)/shard_map/while/body/eval_jaxpr/add | solution.py:35
  94.5 1.7 %fusion.53 = f32[16,8192]{1,0:T(8,128)S(1)} fusion(f32[2,8,64,128]{3,2,1,0:T(8,128)S(1)} %bitcast.136, f32[16,8192]{1,0:T(8,128)S(1)} %get-tuple-element.282, f32[2,8,64,128]{3,2,1,0:T(8,128)S(1)} %bitcast.137, f32[4,16,8192]{2,1,0:T(8,128)} %get-tuple-element.295, s32[]{:T(128)S(6)} %select_n.133), kind=kLoop, calls=%fused_computation.1.clone.1 | loop fusion | flops 393216 | bytes 2621444 | tf_op jit(solution)/shard_map/while/body/eval_jaxpr/add | solution.py:35
  96.6 1.7 %fusion.53 = f32[16,8192]{1,0:T(8,128)S(1)} fusion(f32[2,8,64,128]{3,2,1,0:T(8,128)S(1)} %bitcast.136, f32[16,8192]{1,0:T(8,128)S(1)} %get-tuple-element.282, f32[2,8,64,128]{3,2,1,0:T(8,128)S(1)} %bitcast.137, f32[4,16,8192]{2,1,0:T(8,128)} %get-tuple-element.295, s32[]{:T(128)S(6)} %select_n.133), kind=kLoop, calls=%fused_computation.1.clone.1 | loop fusion | flops 393216 | bytes 2621444 | tf_op jit(solution)/shard_map/while/body/eval_jaxpr/add | solution.py:35
  98.4 0.7 fusion.35
  (36 shorter events, 1.9 us)
Async XLA Ops:
  6.5 8.4 %copy-start.2 = (s32[32]{0:T(128)S(1)}, s32[32]{0:T(128)}, u32[]{:S(2)}) copy-start(s32[32]{0:T(128)} %param.7) | copy-start | bytes 388
  6.5 54.8 %all-gather.6.cloned.1.call-start = ((), (), s32[]{:S(2)}) async-start(), calls=%async_computation | async-start | bytes 2359296 | tf_op jit(solution)/shard_map/all_gather | solution.py:48
  7.3 83.6 %all-gather.8.cloned.1.call-start = ((), (), s32[]{:S(2)}) async-start(), calls=%async_computation.1 | async-start | bytes 2621440 | tf_op jit(solution)/shard_map/all_gather | solution.py:17
  61.3 2.9 %copy-start.1 = (bf16[2,1024,512]{2,1,0:T(8,128)(2,1)S(1)}, bf16[2,1024,512]{2,1,0:T(8,128)(2,1)}, u32[]{:S(2)}) copy-start(bf16[2,1024,512]{2,1,0:T(8,128)(2,1)} %all-gather.6.cloned.1.call-done) | copy-start | bytes 6291460
  65.0 1.2 %copy-start = (f32[16,16,1024]{2,0,1:T(8,128)}, f32[16,16,1024]{2,0,1:T(8,128)S(1)}, u32[]{:S(2)}) copy-start(f32[16,16,1024]{2,0,1:T(8,128)S(1)} %get-tuple-element.217) | copy-start | bytes 3145732
Sparse Core Ops, SparseCore 0:
  9.5 51.7 all-gather.5
  69.5 21.2 all-gather.7
where the time goes:
time: 106 us
  waiting for transfers between devices  54.9 us (52%)
  blocking collectives  18.1 us (17%)
  between operations  13.6 us (13%)
  other arithmetic  9.48 us (9%)
  matrix products  5.18 us (5%)
  local copies, waits for them, and re-layouts  4.54 us (4%)
    all_gather x1, waiting for transfers between devices, per_device(): key_block = lax.all_gather(keys_values, 'qrow', axis=1, tiled=True)  45.9 us
    all_gather x2, blocking collectives, joined(): gathered = jax.tree.map(lambda a: lax.all_gather(a, axis), part)  10.7 us
    all_gather x1, waiting for transfers between devices, joined(): gathered = jax.tree.map(lambda a: lax.all_gather(a, axis), part)  8.29 us
    all_gather x1, blocking collectives, per_device(): row_block = lax.all_gather(queries, 'kcol', axis=0, tiled=True)  7.46 us
    add x3, other arithmetic, combine_parts(): out_one.reshape(height, QUERY_HEADS, HEAD_WIDTH) * scale_one[:, :, None]  5.05 us
    dot_general x4, matrix products, per_device(): jnp.einsum('qhd,kd->hqk', grouped, key_part, preferred_element_type=jnp.f...  3.64 us
    reduce_sum x1, other arithmetic, per_device(): row_sum = jnp.sum(weights, axis=2)  2.33 us
  transfers between devices with their start and end apart: 2, of which 2 were waited for; matrix products, arithmetic and copies ran while one was open for 3% of the time, Pallas kernels for 0%

commit v1 on v0

v1 whole, which is shorter than its diff:
```python
import math

import jax
import jax.numpy as jnp
from jax import lax
from jax.experimental import pallas as pl
from jax.experimental.pallas import tpu as pltpu
from jax.sharding import PartitionSpec as P

QUERY_HEADS = 64
KEY_VALUE_HEADS = 4
HEAD_WIDTH = 128
BLOCK = 128
MESH = pl.DeviceIdType.MESH

masked_score = -1e30


def dot(a, b, dims):
    return lax.dot_general(a, b, (dims, ((), ())), preferred_element_type=jnp.float32)


def make_kernel(rows_n, cols_n, local_rows, blocks_n):
    fold = max(1, 8 // cols_n)
    groups = rows_n // fold
    members = fold * cols_n
    heads = QUERY_HEADS // members
    slice_rows = local_rows * heads
    chunk_rows = members * slice_rows
    devices = rows_n * cols_n
    total_queries = devices * local_rows
    query_blocks = total_queries // BLOCK
    stripe_blocks = blocks_n // query_blocks
    chunk_queries = members * local_rows
    assert BLOCK % chunk_queries == 0 and blocks_n == devices
    first_live = max(0, stripe_blocks - 1 - blocks_n // 2)
    block_of = lambda e, g: (e % cols_n) * rows_n + g * fold + e // cols_n
    spans = [[block_of(e, g) >= first_live for g in range(groups)] for e in range(members)]
    sure = [e for e in range(members) if all(spans[e])]
    maybe = [e for e in range(members) if any(spans[e]) and not all(spans[e])]
    slots = sure + maybe
    scale = 1.0 / math.sqrt(HEAD_WIDTH)

    def where_is(group, member):
        return (group * fold + member // cols_n, member % cols_n)

    def kernel(doc_ref, q_ref, kv_ref, out_ref, qbuf, kvbuf, osend, ssend, obuf, sbuf,
               q_send, q_recv, kv_send, kv_recv, o_send, o_recv, s_send, s_recv):
        row, col = lax.axis_index("qrow"), lax.axis_index("kcol")
        group = row // fold
        member = (row % fold) * cols_n + col
        me = row * cols_n + col
        my_block = col * rows_n + row
        my_slot = sum(i * (member == e).astype(jnp.int32) for i, e in enumerate(slots))

        barrier = pltpu.get_barrier_semaphore()

        @pl.loop(1, devices)
        def _(k):
            other = lax.rem(me + k, devices)
            pl.semaphore_signal(barrier, inc=1, device_id=(other // cols_n, other % cols_n), device_id_type=MESH)

        for i, e in enumerate(maybe):
            @pl.when(block_of(e, group) < first_live)
            def _():
                kvbuf[len(sure) + i] = jnp.zeros((2, BLOCK, HEAD_WIDTH), kvbuf.dtype)

        pl.semaphore_wait(barrier, devices - 1)

        def kv_part(e):
            first = pl.multiple_of(e * heads // (QUERY_HEADS // KEY_VALUE_HEADS) * HEAD_WIDTH, HEAD_WIDTH)
            return kv_ref.at[:, :, pl.ds(first, HEAD_WIDTH)]

        def kv_copy(k):
            e = lax.rem(member + k, members)
            return pltpu.make_async_remote_copy(
                src_ref=kv_part(e), dst_ref=kvbuf.at[my_slot], send_sem=kv_send.at[k],
                recv_sem=kv_recv.at[my_slot], device_id=where_is(group, e), device_id_type=MESH)

        @pl.when(my_block >= first_live)
        def _():
            pltpu.make_async_copy(kv_part(member), kvbuf.at[my_slot], kv_recv.at[my_slot]).start()
            for k in range(1, members):
                kv_copy(k).start()

        pltpu.make_async_copy(q_ref.at[member], qbuf.at[me], q_recv.at[group]).start()

        @pl.loop(1, devices)
        def _(k):
            other = lax.rem(me + k, devices)
            e = lax.rem(other, members)
            pltpu.make_async_remote_copy(
                src_ref=q_ref.at[e], dst_ref=qbuf.at[me], send_sem=q_send, recv_sem=q_recv.at[group],
                device_id=(other // cols_n, other % cols_n), device_id_type=MESH).start()

        for i, e in enumerate(slots):
            wait = pltpu.make_async_copy(kvbuf.at[i], kvbuf.at[i], kv_recv.at[i]).wait
            if e in sure:
                wait()
            else:
                pl.when(block_of(e, group) >= first_live)(wait)

        lane = lax.broadcasted_iota(jnp.int32, (chunk_rows, BLOCK), 1)
        row_index = lax.broadcasted_iota(jnp.int32, (chunk_rows, BLOCK), 0)
        row_query = row_index // heads
        diagonal = (lax.broadcasted_iota(jnp.int32, (slice_rows, BLOCK), 0)
                    == lax.broadcasted_iota(jnp.int32, (slice_rows, BLOCK), 1))

        def attend(source):
            first = source * members
            mine = qbuf.at[pl.ds(first, members)]
            pltpu.make_async_copy(mine, mine, q_recv.at[source]).wait()
            q = qbuf[pl.ds(first, members)].reshape(chunk_rows, HEAD_WIDTH)
            query_first = source * chunk_queries
            query_block = (query_first // BLOCK + 1) * stripe_blocks - 1
            in_block = row_query + query_first % BLOCK
            query_doc = doc_ref[query_block]
            scores = []
            for i, e in enumerate(slots):
                b = block_of(e, group)
                same = doc_ref[b] == query_doc
                whole = jnp.where(same & (b < query_block), BLOCK, -1)
                causal = jnp.where(same & (b == query_block), 0, -2 * BLOCK)
                limit = jnp.maximum(in_block + causal, whole)
                s = dot(q, kvbuf[i, 0], ((1,), (1,))) * scale
                scores.append((s, lane <= limit))
            masked = [jnp.where(live, s, masked_score) for s, live in scores]
            top = masked[0]
            for s in masked[1:]:
                top = jnp.maximum(top, s)
            top = jnp.max(top, axis=1, keepdims=True)
            total = None
            acc = None
            for i in range(len(slots)):
                p = jnp.where(scores[i][1], jnp.exp(masked[i] - top), 0.0)
                total = p if total is None else total + p
                o = dot(p.astype(jnp.bfloat16), kvbuf[i, 1], ((1,), (0,)))
                acc = o if acc is None else acc + o
            total = jnp.sum(total, axis=1, keepdims=True)
            osend[pl.ds(first, members)] = acc.astype(jnp.bfloat16).reshape(members, slice_rows, HEAD_WIDTH)
            for j in range(members):
                part = slice(j * slice_rows, (j + 1) * slice_rows)
                ssend[first + j, 0:1] = jnp.sum(jnp.where(diagonal, top[part], 0.0), axis=0, keepdims=True)
                ssend[first + j, 1:2] = jnp.sum(jnp.where(diagonal, total[part], 0.0), axis=0, keepdims=True)

        def give(source, j):
            k = source * members + j
            return [
                pltpu.make_async_remote_copy(
                    src_ref=src.at[k], dst_ref=dst.at[group, member], send_sem=sent, recv_sem=got.at[group],
                    device_id=where_is(source, j), device_id_type=MESH)
                for src, dst, sent, got in ((osend, obuf, o_send, o_recv), (ssend, sbuf, s_send, s_recv))
            ]

        attend(group)
        pltpu.make_async_copy(osend.at[me], obuf.at[group, member], o_recv.at[group]).start()
        pltpu.make_async_copy(ssend.at[me], sbuf.at[group, member], s_recv.at[group]).start()
        for i in range(1, members):
            for copy in give(group, lax.rem(member + i, members)):
                copy.start()

        @pl.loop(1, groups)
        def _(k):
            source = lax.rem(group + k, groups)
            attend(source)
            for j in range(members):
                for copy in give(source, j):
                    copy.start()

        for g in range(groups):
            pltpu.make_async_copy(sbuf.at[g], sbuf.at[g], s_recv.at[g]).wait()
            pltpu.make_async_copy(obuf.at[g], obuf.at[g], o_recv.at[g]).wait()

        for e in range(members):
            tops = [sbuf[g, e, 0:1] for g in range(groups)]
            overall = tops[0]
            for t in tops[1:]:
                overall = jnp.maximum(overall, t)
            factors = [jnp.exp(t - overall) for t in tops]
            weight = sum(f * sbuf[g, e, 1:2] for g, f in enumerate(factors))
            merged = None
            for g, f in enumerate(factors):
                column = jnp.sum(jnp.where(diagonal, f, 0.0), axis=1, keepdims=True)
                term = column * obuf[g, e].astype(jnp.float32)
                merged = term if merged is None else merged + term
            column = jnp.sum(jnp.where(diagonal, weight, 0.0), axis=1, keepdims=True)
            out_ref[e] = (merged / column).astype(out_ref.dtype)

        @pl.when(my_block >= first_live)
        def _():
            for k in range(1, members):
                kv_copy(k).wait_send()
        others = qbuf.at[pl.ds(0, devices - 1)]
        pltpu.make_async_copy(others, others, q_send).wait()
        others = osend.at[pl.ds(0, devices - 1)]
        pltpu.make_async_copy(others, others, o_send).wait()
        others = ssend.at[pl.ds(0, devices - 1)]
        pltpu.make_async_copy(others, others, s_send).wait()

    bf16, dma = jnp.bfloat16, pltpu.SemaphoreType.DMA
    scratch = [
        pltpu.VMEM((devices, slice_rows, HEAD_WIDTH), bf16),
        pltpu.VMEM((len(slots), 2, BLOCK, HEAD_WIDTH), bf16),
        pltpu.VMEM((devices, slice_rows, HEAD_WIDTH), bf16),
        pltpu.VMEM((devices, 2, BLOCK), jnp.float32),
        pltpu.VMEM((groups, members, slice_rows, HEAD_WIDTH), bf16),
        pltpu.VMEM((groups, members, 2, BLOCK), jnp.float32),
        dma, dma((groups,)), dma((members,)), dma((len(slots),)),
        dma, dma((groups,)), dma, dma((groups,)),
    ]
    return kernel, scratch, members, heads, slice_rows


def solution(mesh):
    rows_n, cols_n = mesh.shape["qrow"], mesh.shape["kcol"]

    def per_device(queries, keys_values, doc_blocks):
        local_rows = queries.shape[0]
        kernel, scratch, members, heads, slice_rows = make_kernel(rows_n, cols_n, local_rows, doc_blocks.shape[0])
        q = queries.reshape(local_rows, members, heads, HEAD_WIDTH).transpose(1, 0, 2, 3)
        q = q.reshape(members, slice_rows, HEAD_WIDTH)
        out = pl.pallas_call(
            kernel,
            out_shape=jax.ShapeDtypeStruct((members, slice_rows, HEAD_WIDTH), jnp.bfloat16),
            in_specs=[
                pl.BlockSpec(memory_space=pltpu.SMEM),
                pl.BlockSpec(memory_space=pl.ANY),
                pl.BlockSpec(memory_space=pl.ANY),
            ],
            out_specs=pl.BlockSpec(memory_space=pltpu.VMEM),
            scratch_shapes=scratch,
            compiler_params=pltpu.CompilerParams(collective_id=0, has_side_effects=True),
        )(doc_blocks, q, keys_values)
        out = out.reshape(members, local_rows, heads, HEAD_WIDTH).transpose(1, 0, 2, 3)
        return out.reshape(local_rows, QUERY_HEADS * HEAD_WIDTH)

    return jax.shard_map(
        per_device,
        mesh=mesh,
        in_specs=(P(("qrow", "kcol"), None), P(None, ("kcol", "qrow"), None), P()),
        out_specs=P(("qrow", "kcol"), None),
        check_vma=False,
    )
```

time: 106 us -> 30 us (0.28)
  waiting for transfers between devices: 54.9 us -> 0 us
  Pallas kernels: 0 us -> 26.7 us
  blocking collectives: 18.1 us -> 0 us
  between operations: 13.6 us -> 0.01 us
  other arithmetic: 9.48 us -> 0 us
  matrix products: 5.18 us -> 0 us
  local copies, waits for them, and re-layouts: 4.54 us -> 3.01 us
    all_gather x2 -> x0, waiting for transfers between devices: 54.2 us -> none  [the longest x1 45.9 us: per_device(): key_block = lax.all_gather(keys_values, 'qrow', axis=1, tiled=True)]
    pallas_call x0 -> x1, Pallas kernels: none -> 26.7 us  [per_device(): pl.pallas_call(kernel, out_shape=jax.ShapeDtypeStruct((members, slice_row...]
    all_gather x3 -> x0, blocking collectives: 18.1 us -> none  [the longest x2 10.7 us: joined(): gathered = jax.tree.map(lambda a: lax.all_gather(a, axis), part)]
    dot_general x8 -> x0, matrix products: 5.18 us -> none  [the longest x4 3.64 us: per_device(): jnp.einsum('qhd,kd->hqk', grouped, key_part, preferred_element_type=jnp.f...]
    add x8 -> x0, other arithmetic: 5.12 us -> none  [the longest x3 5.05 us: combine_parts(): out_one.reshape(height, QUERY_HEADS, HEAD_WIDTH) * scale_one[:, :, None]]
    reduce_sum x2 -> x0, other arithmetic: 2.51 us -> none  [the longest x1 2.33 us: per_device(): row_sum = jnp.sum(weights, axis=2)]
    another operation x1 -> x0, local copies, waits for them, and re-layouts: 1.93 us -> none  [joined(): gathered = jax.tree.map(lambda a: lax.all_gather(a, axis), part)]
    reshape x0 -> x1, local copies, waits for them, and re-layouts: none -> 1.48 us  [per_device(): q = q.reshape(members, slice_rows, HEAD_WIDTH)]
  transfers between devices with their start and end apart: 2 -> 0, of which waited for: 2 -> 0; matrix products, arithmetic and copies ran while one was open for 3% -> 0% of each run, Pallas kernels for 0% -> 0%
where the time goes in v1:
time: 30 us; the launch traced here: 29.8 us
  Pallas kernels  26.7 us (89%)
  local copies, waits for them, and re-layouts  3.01 us (10%)
    pallas_call x1, Pallas kernels, per_device(): pl.pallas_call(kernel, out_shape=jax.ShapeDtypeStruct((members, slice_row...  26.7 us
    unnamed x2, local copies, waits for them, and re-layouts  1.54 us
    reshape x1, local copies, waits for them, and re-layouts, per_device(): q = q.reshape(members, slice_rows, HEAD_WIDTH)  1.48 us

profile of v1, /device:TPU:0, one launch (start us, length us, event | category | flops | bytes accessed | tf_op | source)
XLA Modules:
  0.0 29.8 jit_solution(18180696970749153121)
XLA Ops:
  0.0 1.5 %copy_bitcast_fusion.3.q_ref = bf16[8,32,128]{2,1,0:T(8,128)(2,1)} fusion(bf16[1,4,64,128]{3,1,2,0:T(4,128)(2,1)} %bitcast.20), kind=kLoop, calls=%fused_computation.3 | loop fusion | bytes 131072 | tf_op jit(solution)/shard_map/reshape | solution.py:221
  1.5 26.7 %shard_map.37 = bf16[8,32,128]{2,1,0:T(8,128)(2,1)} custom-call(s32[32]{0:T(128)} %doc_ref.1, bf16[8,32,128]{2,1,0:T(8,128)(2,1)} %copy_bitcast_fusion.3.q_ref, bf16[2,128,512]{2,1,0:T(8,128)(2,1)} %kv_ref.1), custom_call_target="tpu_custom_call" | custom-call | tf_op jit(solution)/shard_map/pallas_call | solution.py:222
  28.2 0.9 %copy_bitcast_fusion.2 = bf16[1,4,64,128]{3,2,1,0:T(8,128)(2,1)S(1)} fusion(bf16[8,32,128]{2,1,0:T(8,128)(2,1)} %shard_map.37), kind=kLoop, calls=%fused_computation.2 | loop fusion | bytes 131072
  29.1 0.7 %copy.13 = bf16[1,4,64,128]{3,1,2,0:T(4,128)(2,1)} copy(bf16[1,4,64,128]{3,2,1,0:T(8,128)(2,1)S(1)} %copy_bitcast_fusion.2) | data formatting | bytes 131072

commit v2 on v1

--- a/solution.py
+++ b/solution.py
@@ -32,7 +32,7 @@
     query_blocks = total_queries // BLOCK
     stripe_blocks = blocks_n // query_blocks
     chunk_queries = members * local_rows
-    assert BLOCK % chunk_queries == 0 and blocks_n == devices
+    assert BLOCK % chunk_queries == 0 and blocks_n == devices and cols_n % 2 == 0 and 2 * slice_rows <= BLOCK
     first_live = max(0, stripe_blocks - 1 - blocks_n // 2)
     block_of = lambda e, g: (e % cols_n) * rows_n + g * fold + e // cols_n
     spans = [[block_of(e, g) >= first_live for g in range(groups)] for e in range(members)]
@@ -44,8 +44,8 @@
     def where_is(group, member):
         return (group * fold + member // cols_n, member % cols_n)
 
-    def kernel(doc_ref, q_ref, kv_ref, out_ref, qbuf, kvbuf, osend, ssend, obuf, sbuf,
-               q_send, q_recv, kv_send, kv_recv, o_send, o_recv, s_send, s_recv):
+    def kernel(doc_ref, q_ref, kv_ref, out_ref, qsend, wide, qbuf, kvbuf, osend, ssend, obuf, sbuf,
+               q_send, q_recv, kv_send, kv_recv, pair_send, pair_recv, o_send, o_recv, s_send, s_recv):
         row, col = lax.axis_index("qrow"), lax.axis_index("kcol")
         group = row // fold
         member = (row % fold) * cols_n + col
@@ -53,6 +53,7 @@
         my_block = col * rows_n + row
         my_slot = sum(i * (member == e).astype(jnp.int32) for i, e in enumerate(slots))
 
+        half = lax.rem(member, 2)
         barrier = pltpu.get_barrier_semaphore()
 
         @pl.loop(1, devices)
@@ -65,46 +66,65 @@
             def _():
                 kvbuf[len(sure) + i] = jnp.zeros((2, BLOCK, HEAD_WIDTH), kvbuf.dtype)
 
+        for e in range(members):
+            for h in range(heads):
+                first = (e * heads + h) * HEAD_WIDTH
+                wide[e, h * local_rows:(h + 1) * local_rows] = q_ref[:, first:first + HEAD_WIDTH].astype(jnp.float32)
+            qsend[e] = wide[e].astype(qsend.dtype)
+
         pl.semaphore_wait(barrier, devices - 1)
 
         def kv_part(e):
             first = pl.multiple_of(e * heads // (QUERY_HEADS // KEY_VALUE_HEADS) * HEAD_WIDTH, HEAD_WIDTH)
-            return kv_ref.at[:, :, pl.ds(first, HEAD_WIDTH)]
+            return kv_ref.at[lax.rem(e, 2), :, pl.ds(first, HEAD_WIDTH)]
 
         def kv_copy(k):
             e = lax.rem(member + k, members)
             return pltpu.make_async_remote_copy(
-                src_ref=kv_part(e), dst_ref=kvbuf.at[my_slot], send_sem=kv_send.at[k],
+                src_ref=kv_part(e), dst_ref=kvbuf.at[my_slot, lax.rem(e, 2)], send_sem=kv_send.at[k],
                 recv_sem=kv_recv.at[my_slot], device_id=where_is(group, e), device_id_type=MESH)
 
         @pl.when(my_block >= first_live)
         def _():
-            pltpu.make_async_copy(kv_part(member), kvbuf.at[my_slot], kv_recv.at[my_slot]).start()
+            pltpu.make_async_copy(kv_part(member), kvbuf.at[my_slot, half], kv_recv.at[my_slot]).start()
             for k in range(1, members):
                 kv_copy(k).start()
 
-        pltpu.make_async_copy(q_ref.at[member], qbuf.at[me], q_recv.at[group]).start()
+        pltpu.make_async_copy(qsend.at[member], qbuf.at[me], q_recv.at[group]).start()
 
         @pl.loop(1, devices)
         def _(k):
             other = lax.rem(me + k, devices)
             e = lax.rem(other, members)
             pltpu.make_async_remote_copy(
-                src_ref=q_ref.at[e], dst_ref=qbuf.at[me], send_sem=q_send, recv_sem=q_recv.at[group],
+                src_ref=qsend.at[e], dst_ref=qbuf.at[me], send_sem=q_send, recv_sem=q_recv.at[group],
                 device_id=(other // cols_n, other % cols_n), device_id_type=MESH).start()
 
-        for i, e in enumerate(slots):
-            wait = pltpu.make_async_copy(kvbuf.at[i], kvbuf.at[i], kv_recv.at[i]).wait
-            if e in sure:
-                wait()
-            else:
-                pl.when(block_of(e, group) >= first_live)(wait)
+        def pair_copy(i):
+            return pltpu.make_async_remote_copy(
+                src_ref=kvbuf.at[i, half], dst_ref=kvbuf.at[i, half], send_sem=pair_send.at[i],
+                recv_sem=pair_recv.at[i], device_id=(row, col + 1 - 2 * lax.rem(col, 2)), device_id_type=MESH)
+
+        def per_slot(step):
+            for i, e in enumerate(slots):
+                if e in sure:
+                    step(i)
+                else:
+                    pl.when(block_of(e, group) >= first_live)(lambda: step(i))
+
+        def pass_on(i):
+            pltpu.make_async_copy(kvbuf.at[i, half], kvbuf.at[i, half], kv_recv.at[i]).wait()
+            pair_copy(i).start()
+
+        per_slot(pass_on)
+        per_slot(lambda i: pair_copy(i).wait_recv())
 
         lane = lax.broadcasted_iota(jnp.int32, (chunk_rows, BLOCK), 1)
         row_index = lax.broadcasted_iota(jnp.int32, (chunk_rows, BLOCK), 0)
-        row_query = row_index // heads
-        diagonal = (lax.broadcasted_iota(jnp.int32, (slice_rows, BLOCK), 0)
-                    == lax.broadcasted_iota(jnp.int32, (slice_rows, BLOCK), 1))
+        row_query = row_index // slice_rows * local_rows + row_index % local_rows
+        offset = (lax.broadcasted_iota(jnp.int32, (slice_rows, BLOCK), 1)
+                  - lax.broadcasted_iota(jnp.int32, (slice_rows, BLOCK), 0))
+        top_place, total_place = offset == 0, offset == slice_rows
 
         def attend(source):
             first = source * members
@@ -140,8 +160,8 @@
             osend[pl.ds(first, members)] = acc.astype(jnp.bfloat16).reshape(members, slice_rows, HEAD_WIDTH)
             for j in range(members):
                 part = slice(j * slice_rows, (j + 1) * slice_rows)
-                ssend[first + j, 0:1] = jnp.sum(jnp.where(diagonal, top[part], 0.0), axis=0, keepdims=True)
-                ssend[first + j, 1:2] = jnp.sum(jnp.where(diagonal, total[part], 0.0), axis=0, keepdims=True)
+                stats = jnp.where(top_place, top[part], jnp.where(total_place, total[part], 0.0))
+                ssend[first + j] = jnp.sum(stats, axis=0, keepdims=True)
 
         def give(source, j):
             k = source * members + j
@@ -172,19 +192,24 @@
             pltpu.make_async_copy(obuf.at[g], obuf.at[g], o_recv.at[g]).wait()
 
         for e in range(members):
-            tops = [sbuf[g, e, 0:1] for g in range(groups)]
+            column = lambda g, place: jnp.sum(jnp.where(place, sbuf[g, e], 0.0), axis=1, keepdims=True)
+            tops = [column(g, top_place) for g in range(groups)]
             overall = tops[0]
             for t in tops[1:]:
                 overall = jnp.maximum(overall, t)
-            factors = [jnp.exp(t - overall) for t in tops]
-            weight = sum(f * sbuf[g, e, 1:2] for g, f in enumerate(factors))
-            merged = None
-            for g, f in enumerate(factors):
-                column = jnp.sum(jnp.where(diagonal, f, 0.0), axis=1, keepdims=True)
-                term = column * obuf[g, e].astype(jnp.float32)
+            merged = weight = None
+            for g in range(groups):
+                factor = jnp.exp(tops[g] - overall)
+                term = factor * obuf[g, e].astype(jnp.float32)
+                part = factor * column(g, total_place)
                 merged = term if merged is None else merged + term
-            column = jnp.sum(jnp.where(diagonal, weight, 0.0), axis=1, keepdims=True)
-            out_ref[e] = (merged / column).astype(out_ref.dtype)
+                weight = part if weight is None else weight + part
+            wide[e] = merged / weight
+            for h in range(heads):
+                first = (e * heads + h) * HEAD_WIDTH
+                out_ref[:, first:first + HEAD_WIDTH] = wide[e, h * local_rows:(h + 1) * local_rows].astype(out_ref.dtype)
+
+        per_slot(lambda i: pair_copy(i).wait_send())
 
         @pl.when(my_block >= first_live)
         def _():
@@ -199,16 +224,18 @@
 
     bf16, dma = jnp.bfloat16, pltpu.SemaphoreType.DMA
     scratch = [
+        pltpu.VMEM((members, slice_rows, HEAD_WIDTH), bf16),
+        pltpu.VMEM((members, slice_rows, HEAD_WIDTH), jnp.float32),
         pltpu.VMEM((devices, slice_rows, HEAD_WIDTH), bf16),
         pltpu.VMEM((len(slots), 2, BLOCK, HEAD_WIDTH), bf16),
         pltpu.VMEM((devices, slice_rows, HEAD_WIDTH), bf16),
-        pltpu.VMEM((devices, 2, BLOCK), jnp.float32),
+        pltpu.VMEM((devices, 1, BLOCK), jnp.float32),
         pltpu.VMEM((groups, members, slice_rows, HEAD_WIDTH), bf16),
-        pltpu.VMEM((groups, members, 2, BLOCK), jnp.float32),
-        dma, dma((groups,)), dma((members,)), dma((len(slots),)),
+        pltpu.VMEM((groups, members, 1, BLOCK), jnp.float32),
+        dma, dma((groups,)), dma((members,)), dma((len(slots),)), dma((len(slots),)), dma((len(slots),)),
         dma, dma((groups,)), dma, dma((groups,)),
     ]
-    return kernel, scratch, members, heads, slice_rows
+    return kernel, scratch
 
 
 def solution(mesh):
@@ -216,23 +243,19 @@
 
     def per_device(queries, keys_values, doc_blocks):
         local_rows = queries.shape[0]
-        kernel, scratch, members, heads, slice_rows = make_kernel(rows_n, cols_n, local_rows, doc_blocks.shape[0])
-        q = queries.reshape(local_rows, members, heads, HEAD_WIDTH).transpose(1, 0, 2, 3)
-        q = q.reshape(members, slice_rows, HEAD_WIDTH)
-        out = pl.pallas_call(
+        kernel, scratch = make_kernel(rows_n, cols_n, queries.shape[0], doc_blocks.shape[0])
+        return pl.pallas_call(
             kernel,
-            out_shape=jax.ShapeDtypeStruct((members, slice_rows, HEAD_WIDTH), jnp.bfloat16),
+            out_shape=jax.ShapeDtypeStruct(queries.shape, queries.dtype),
             in_specs=[
                 pl.BlockSpec(memory_space=pltpu.SMEM),
-                pl.BlockSpec(memory_space=pl.ANY),
+                pl.BlockSpec(memory_space=pltpu.VMEM),
                 pl.BlockSpec(memory_space=pl.ANY),
             ],
             out_specs=pl.BlockSpec(memory_space=pltpu.VMEM),
             scratch_shapes=scratch,
             compiler_params=pltpu.CompilerParams(collective_id=0, has_side_effects=True),
-        )(doc_blocks, q, keys_values)
-        out = out.reshape(members, local_rows, heads, HEAD_WIDTH).transpose(1, 0, 2, 3)
-        return out.reshape(local_rows, QUERY_HEADS * HEAD_WIDTH)
+        )(doc_blocks, queries, keys_values)
 
     return jax.shard_map(
         per_device,

time: 30 us -> 26.4 us (0.88)
  Pallas kernels: 26.7 us -> 24.6 us
  local copies, waits for them, and re-layouts: 3.01 us -> 1.49 us
    pallas_call x1, Pallas kernels: 26.7 us -> 24.6 us  [per_device(): pl.pallas_call(kernel, out_shape=jax.ShapeDtypeStruct(queries.shape, quer...]
    reshape x1 -> x0, local copies, waits for them, and re-layouts: 1.48 us -> none  [per_device(): q = q.reshape(members, slice_rows, HEAD_WIDTH)]
    unnamed x2 -> x1, local copies, waits for them, and re-layouts: 1.54 us -> 1.49 us
where the time goes in v2:
time: 26.4 us; the launch traced here: 26.2 us
  Pallas kernels  24.6 us (93%)
  local copies, waits for them, and re-layouts  1.49 us (6%)
    pallas_call x1, Pallas kernels, per_device(): pl.pallas_call(kernel, out_shape=jax.ShapeDtypeStruct(queries.shape, quer...  24.6 us
    unnamed x1, local copies, waits for them, and re-layouts  1.49 us

profile of v2, /device:TPU:0, one launch (start us, length us, event | category | flops | bytes accessed | tf_op | source)
XLA Modules:
  0.0 26.2 jit_solution(12855975281700897114)
XLA Ops:
  0.0 24.6 %shard_map.37 = bf16[4,8192]{1,0:T(4,128)(2,1)} custom-call(s32[32]{0:T(128)} %doc_ref.1, bf16[4,8192]{1,0:T(4,128)(2,1)} %q_ref.1, bf16[2,128,512]{2,1,0:T(8,128)(2,1)} %kv_ref.1), custom_call_target="tpu_custom_call" | custom-call | tf_op jit(solution)/shard_map/pallas_call | solution.py:247
  24.7 1.5 %copy.5 = bf16[4,8192]{1,0:T(4,128)(2,1)} copy(bf16[4,8192]{1,0:T(4,128)(2,1)} %shard_map.37) | data formatting | bytes 131072

commit v3 on v2

--- a/solution.py
+++ b/solution.py
@@ -39,12 +39,20 @@
     sure = [e for e in range(members) if all(spans[e])]
     maybe = [e for e in range(members) if any(spans[e]) and not all(spans[e])]
     slots = sure + maybe
-    scale = 1.0 / math.sqrt(HEAD_WIDTH)
+    scale = math.log2(math.e) / math.sqrt(HEAD_WIDTH)
+
+    apart = max(1, groups // 2)
+
+    def visited(group, k):
+        block = group // apart
+        far = lax.rem(block + 1, groups // apart) * apart + lax.rem(group + k, apart)
+        near = block * apart + lax.rem(group + k - apart, apart)
+        return jnp.where(k == 0, group, jnp.where(k <= apart, far, near))
 
     def where_is(group, member):
         return (group * fold + member // cols_n, member % cols_n)
 
-    def kernel(doc_ref, q_ref, kv_ref, out_ref, qsend, wide, qbuf, kvbuf, osend, ssend, obuf, sbuf,
+    def kernel(doc_ref, q_ref, kv_ref, out_ref, local, local_sem, qsend, wide, qbuf, kvbuf, osend, ssend, obuf, sbuf,
                q_send, q_recv, kv_send, kv_recv, pair_send, pair_recv, o_send, o_recv, s_send, s_recv):
         row, col = lax.axis_index("qrow"), lax.axis_index("kcol")
         group = row // fold
@@ -56,6 +64,9 @@
         half = lax.rem(member, 2)
         barrier = pltpu.get_barrier_semaphore()
 
+        fetch = pltpu.make_async_copy(kv_ref, local, local_sem)
+        fetch.start()
+
         @pl.loop(1, devices)
         def _(k):
             other = lax.rem(me + k, devices)
@@ -64,7 +75,7 @@
         for i, e in enumerate(maybe):
             @pl.when(block_of(e, group) < first_live)
             def _():
-                kvbuf[len(sure) + i] = jnp.zeros((2, BLOCK, HEAD_WIDTH), kvbuf.dtype)
+                kvbuf[:, len(sure) + i] = jnp.zeros((2, BLOCK, HEAD_WIDTH), kvbuf.dtype)
 
         for e in range(members):
             for h in range(heads):
@@ -72,21 +83,22 @@
                 wide[e, h * local_rows:(h + 1) * local_rows] = q_ref[:, first:first + HEAD_WIDTH].astype(jnp.float32)
             qsend[e] = wide[e].astype(qsend.dtype)
 
+        fetch.wait()
         pl.semaphore_wait(barrier, devices - 1)
 
         def kv_part(e):
             first = pl.multiple_of(e * heads // (QUERY_HEADS // KEY_VALUE_HEADS) * HEAD_WIDTH, HEAD_WIDTH)
-            return kv_ref.at[lax.rem(e, 2), :, pl.ds(first, HEAD_WIDTH)]
+            return local.at[lax.rem(e, 2), :, pl.ds(first, HEAD_WIDTH)]
 
         def kv_copy(k):
             e = lax.rem(member + k, members)
             return pltpu.make_async_remote_copy(
-                src_ref=kv_part(e), dst_ref=kvbuf.at[my_slot, lax.rem(e, 2)], send_sem=kv_send.at[k],
+                src_ref=kv_part(e), dst_ref=kvbuf.at[lax.rem(e, 2), my_slot], send_sem=kv_send.at[k],
                 recv_sem=kv_recv.at[my_slot], device_id=where_is(group, e), device_id_type=MESH)
 
         @pl.when(my_block >= first_live)
         def _():
-            pltpu.make_async_copy(kv_part(member), kvbuf.at[my_slot, half], kv_recv.at[my_slot]).start()
+            pltpu.make_async_copy(kv_part(member), kvbuf.at[half, my_slot], kv_recv.at[my_slot]).start()
             for k in range(1, members):
                 kv_copy(k).start()
 
@@ -94,15 +106,14 @@
 
         @pl.loop(1, devices)
         def _(k):
-            other = lax.rem(me + k, devices)
-            e = lax.rem(other, members)
+            e = lax.rem(member + k, members)
             pltpu.make_async_remote_copy(
                 src_ref=qsend.at[e], dst_ref=qbuf.at[me], send_sem=q_send, recv_sem=q_recv.at[group],
-                device_id=(other // cols_n, other % cols_n), device_id_type=MESH).start()
+                device_id=where_is(visited(group, k // members), e), device_id_type=MESH).start()
 
         def pair_copy(i):
             return pltpu.make_async_remote_copy(
-                src_ref=kvbuf.at[i, half], dst_ref=kvbuf.at[i, half], send_sem=pair_send.at[i],
+                src_ref=kvbuf.at[half, i], dst_ref=kvbuf.at[half, i], send_sem=pair_send.at[i],
                 recv_sem=pair_recv.at[i], device_id=(row, col + 1 - 2 * lax.rem(col, 2)), device_id_type=MESH)
 
         def per_slot(step):
@@ -113,7 +124,7 @@
                     pl.when(block_of(e, group) >= first_live)(lambda: step(i))
 
         def pass_on(i):
-            pltpu.make_async_copy(kvbuf.at[i, half], kvbuf.at[i, half], kv_recv.at[i]).wait()
+            pltpu.make_async_copy(kvbuf.at[half, i], kvbuf.at[half, i], kv_recv.at[i]).wait()
             pair_copy(i).start()
 
         per_slot(pass_on)
@@ -135,28 +146,27 @@
             query_block = (query_first // BLOCK + 1) * stripe_blocks - 1
             in_block = row_query + query_first % BLOCK
             query_doc = doc_ref[query_block]
-            scores = []
+            keys = kvbuf[0].reshape(len(slots) * BLOCK, HEAD_WIDTH)
+            values = kvbuf[1].reshape(len(slots) * BLOCK, HEAD_WIDTH)
+            scores = dot(q, keys, ((1,), (1,)))
+            masked = []
             for i, e in enumerate(slots):
                 b = block_of(e, group)
                 same = doc_ref[b] == query_doc
                 whole = jnp.where(same & (b < query_block), BLOCK, -1)
                 causal = jnp.where(same & (b == query_block), 0, -2 * BLOCK)
                 limit = jnp.maximum(in_block + causal, whole)
-                s = dot(q, kvbuf[i, 0], ((1,), (1,))) * scale
-                scores.append((s, lane <= limit))
-            masked = [jnp.where(live, s, masked_score) for s, live in scores]
+                masked.append(jnp.where(lane <= limit, scores[:, i * BLOCK:(i + 1) * BLOCK], masked_score))
             top = masked[0]
             for s in masked[1:]:
                 top = jnp.maximum(top, s)
-            top = jnp.max(top, axis=1, keepdims=True)
-            total = None
-            acc = None
-            for i in range(len(slots)):
-                p = jnp.where(scores[i][1], jnp.exp(masked[i] - top), 0.0)
-                total = p if total is None else total + p
-                o = dot(p.astype(jnp.bfloat16), kvbuf[i, 1], ((1,), (0,)))
-                acc = o if acc is None else acc + o
+            top = jnp.maximum(jnp.max(top, axis=1, keepdims=True), 0.5 * masked_score)
+            weights = [jnp.exp2((s - top) * scale) for s in masked]
+            total = weights[0]
+            for p in weights[1:]:
+                total = total + p
             total = jnp.sum(total, axis=1, keepdims=True)
+            acc = dot(jnp.concatenate([p.astype(jnp.bfloat16) for p in weights], axis=1), values, ((1,), (0,)))
             osend[pl.ds(first, members)] = acc.astype(jnp.bfloat16).reshape(members, slice_rows, HEAD_WIDTH)
             for j in range(members):
                 part = slice(j * slice_rows, (j + 1) * slice_rows)
@@ -199,7 +209,7 @@
                 overall = jnp.maximum(overall, t)
             merged = weight = None
             for g in range(groups):
-                factor = jnp.exp(tops[g] - overall)
+                factor = jnp.exp2((tops[g] - overall) * scale)
                 term = factor * obuf[g, e].astype(jnp.float32)
                 part = factor * column(g, total_place)
                 merged = term if merged is None else merged + term
@@ -224,10 +234,12 @@
 
     bf16, dma = jnp.bfloat16, pltpu.SemaphoreType.DMA
     scratch = [
+        pltpu.VMEM((2, BLOCK, KEY_VALUE_HEADS * HEAD_WIDTH), bf16),
+        dma,
         pltpu.VMEM((members, slice_rows, HEAD_WIDTH), bf16),
         pltpu.VMEM((members, slice_rows, HEAD_WIDTH), jnp.float32),
         pltpu.VMEM((devices, slice_rows, HEAD_WIDTH), bf16),
-        pltpu.VMEM((len(slots), 2, BLOCK, HEAD_WIDTH), bf16),
+        pltpu.VMEM((2, len(slots), BLOCK, HEAD_WIDTH), bf16),
         pltpu.VMEM((devices, slice_rows, HEAD_WIDTH), bf16),
         pltpu.VMEM((devices, 1, BLOCK), jnp.float32),
         pltpu.VMEM((groups, members, slice_rows, HEAD_WIDTH), bf16),

time: 26.4 us -> 25.2 us (0.955)
  Pallas kernels: 24.6 us -> 23.5 us
    pallas_call x1, Pallas kernels: 24.6 us -> 23.5 us  [per_device(): pl.pallas_call(kernel, out_shape=jax.ShapeDtypeStruct(queries.shape, quer...]
where the time goes in v3:
time: 25.2 us; the launch traced here: 25 us
  Pallas kernels  23.5 us (93%)
  local copies, waits for them, and re-layouts  1.49 us (6%)
    pallas_call x1, Pallas kernels, per_device(): pl.pallas_call(kernel, out_shape=jax.ShapeDtypeStruct(queries.shape, quer...  23.5 us
    unnamed x1, local copies, waits for them, and re-layouts  1.49 us

profile of v3, /device:TPU:0, one launch (start us, length us, event | category | flops | bytes accessed | tf_op | source)
XLA Modules:
  0.0 25.0 jit_solution(2481021580354173114)
XLA Ops:
  0.0 23.5 %shard_map.37 = bf16[4,8192]{1,0:T(4,128)(2,1)} custom-call(s32[32]{0:T(128)} %doc_ref.1, bf16[4,8192]{1,0:T(4,128)(2,1)} %q_ref.1, bf16[2,128,512]{2,1,0:T(8,128)(2,1)} %kv_ref.1), custom_call_target="tpu_custom_call" | custom-call | tf_op jit(solution)/shard_map/pallas_call | solution.py:259
  23.5 1.5 %copy.5 = bf16[4,8192]{1,0:T(4,128)(2,1)} copy(bf16[4,8192]{1,0:T(4,128)(2,1)} %shard_map.37) | data formatting | bytes 131072

commit v4 on v3

--- a/solution.py
+++ b/solution.py
@@ -182,13 +182,6 @@
                 for src, dst, sent, got in ((osend, obuf, o_send, o_recv), (ssend, sbuf, s_send, s_recv))
             ]
 
-        attend(group)
-        pltpu.make_async_copy(osend.at[me], obuf.at[group, member], o_recv.at[group]).start()
-        pltpu.make_async_copy(ssend.at[me], sbuf.at[group, member], s_recv.at[group]).start()
-        for i in range(1, members):
-            for copy in give(group, lax.rem(member + i, members)):
-                copy.start()
-
         @pl.loop(1, groups)
         def _(k):
             source = lax.rem(group + k, groups)
@@ -196,6 +189,13 @@
             for j in range(members):
                 for copy in give(source, j):
                     copy.start()
+
+        attend(group)
+        pltpu.make_async_copy(osend.at[me], obuf.at[group, member], o_recv.at[group]).start()
+        pltpu.make_async_copy(ssend.at[me], sbuf.at[group, member], s_recv.at[group]).start()
+        for i in range(1, members):
+            for copy in give(group, lax.rem(member + i, members)):
+                copy.start()
 
         for g in range(groups):
             pltpu.make_async_copy(sbuf.at[g], sbuf.at[g], s_recv.at[g]).wait()

time: 25.2 us -> 24.9 us (0.988)
  Pallas kernels: 23.5 us -> 23.2 us
    pallas_call x1, Pallas kernels: 23.5 us -> 23.2 us  [per_device(): pl.pallas_call(kernel, out_shape=jax.ShapeDtypeStruct(queries.shape, quer...]
where the time goes in v4:
time: 24.9 us; the launch traced here: 24.7 us
  Pallas kernels  23.2 us (93%)
  local copies, waits for them, and re-layouts  1.49 us (6%)
    pallas_call x1, Pallas kernels, per_device(): pl.pallas_call(kernel, out_shape=jax.ShapeDtypeStruct(queries.shape, quer...  23.2 us
    unnamed x1, local copies, waits for them, and re-layouts  1.49 us

profile of v4, /device:TPU:0, one launch (start us, length us, event | category | flops | bytes accessed | tf_op | source)
XLA Modules:
  0.0 24.7 jit_solution(9652560160526107261)
XLA Ops:
  0.0 23.2 %shard_map.37 = bf16[4,8192]{1,0:T(4,128)(2,1)} custom-call(s32[32]{0:T(128)} %doc_ref.1, bf16[4,8192]{1,0:T(4,128)(2,1)} %q_ref.1, bf16[2,128,512]{2,1,0:T(8,128)(2,1)} %kv_ref.1), custom_call_target="tpu_custom_call" | custom-call | tf_op jit(solution)/shard_map/pallas_call | solution.py:259
  23.2 1.5 %copy.5 = bf16[4,8192]{1,0:T(4,128)(2,1)} copy(bf16[4,8192]{1,0:T(4,128)(2,1)} %shard_map.37) | data formatting | bytes 131072

commit v5 on v4

--- a/solution.py
+++ b/solution.py
@@ -182,13 +182,18 @@
                 for src, dst, sent, got in ((osend, obuf, o_send, o_recv), (ssend, sbuf, s_send, s_recv))
             ]
 
-        @pl.loop(1, groups)
-        def _(k):
+        def step(k):
             source = lax.rem(group + k, groups)
             attend(source)
             for j in range(members):
                 for copy in give(source, j):
                     copy.start()
+
+        if groups <= 4:
+            for k in range(1, groups):
+                step(k)
+        else:
+            pl.loop(1, groups)(step)
 
         attend(group)
         pltpu.make_async_copy(osend.at[me], obuf.at[group, member], o_recv.at[group]).start()

time: 24.9 us -> 24.9 us (level)
  no operation moved by 1% of the time
where the time goes in v5:
time: 24.9 us; the launch traced here: 24.6 us
  Pallas kernels  23.1 us (93%)
  local copies, waits for them, and re-layouts  1.49 us (6%)
    pallas_call x1, Pallas kernels, per_device(): pl.pallas_call(kernel, out_shape=jax.ShapeDtypeStruct(queries.shape, quer...  23.1 us
    unnamed x1, local copies, waits for them, and re-layouts  1.49 us

profile of v5, /device:TPU:0, one launch (start us, length us, event | category | flops | bytes accessed | tf_op | source)
XLA Modules:
  0.0 24.6 jit_solution(2392125576509879503)
XLA Ops:
  0.0 23.1 %shard_map.37 = bf16[4,8192]{1,0:T(4,128)(2,1)} custom-call(s32[32]{0:T(128)} %doc_ref.1, bf16[4,8192]{1,0:T(4,128)(2,1)} %q_ref.1, bf16[2,128,512]{2,1,0:T(8,128)(2,1)} %kv_ref.1), custom_call_target="tpu_custom_call" | custom-call | tf_op jit(solution)/shard_map/pallas_call | solution.py:264
  23.2 1.5 %copy.5 = bf16[4,8192]{1,0:T(4,128)(2,1)} copy(bf16[4,8192]{1,0:T(4,128)(2,1)} %shard_map.37) | data formatting | bytes 131072
